TPU v7x, 128 devices: a whole 4x4x4 slice. The times are simulated.
128 devices in a mesh: sens: 8 (over z, core), layer: 16 (over y, x).
Axes of the slice: x: 4, y: 4, z: 4, core: 2. Of those that a mesh axis runs over, the one named last changes fastest.
Arguments:
- slopes: bfloat16 [1024, 63600], P('layer', 'sens'), may hold values from -7 to 7
- valid: int32 [63600], P('sens'), may hold values from 0 to 1
- sensor_map: int32 [63600], P('sens'), may hold values from 0 to 5, as said below
- reconstructor: bfloat16 [16000, 63600], P('layer', 'sens'), may hold values from -0.0234375 to 0.0234375
- fitting: bfloat16 [7800, 16000], P('sens', 'layer'), may hold values from -0.046875 to 0.046875
Outputs:
- commands: float32 [1024, 7800], P(('sens', 'layer'))
Inputs may be any that keep to these rules, and one draw needn't show every extreme that they name: `sensor_map`: both slopes of a subaperture (indices 2 i and 2 i + 1) belong to one sensor.
All inputs are finite; a program needn't handle non-finite values.
Results may differ from a plain program's by a relative error of at most 0.02.
Values may be sent and summed in bfloat16 or wider, within the bound.
No kernel may reach another device: no remote copies, remote signals or barrier semaphores. Data moves between devices by JAX's collectives and lax.ppermute only.
A program may use at most 192 MiB of HBM per device.

v0:
```python
import jax
import jax.numpy as jnp
from jax import lax
from jax.sharding import PartitionSpec as P

SENSORS = 6


def copy_for_each(x, axis):
    length = lax.axis_size(axis)
    return lax.all_to_all(jnp.broadcast_to(x[None], (length, *x.shape)), axis, 0, 0, tiled=True)


def taken_together(x, axis):
    everything = copy_for_each(x, axis)
    return jnp.sum(everything.astype(jnp.float32), axis=0)


def cut_along(x, dim, length):
    dims = x.shape
    blocks = x.reshape(*dims[:dim], length, dims[dim] // length, *dims[dim + 1 :])
    return jnp.moveaxis(blocks, dim, 0)


def summed_on_arrival(x, axis, dim):
    blocks = cut_along(x, dim, lax.axis_size(axis))
    arrived = lax.all_to_all(blocks, axis, split_axis=0, concat_axis=0, tiled=True)
    return arrived.astype(jnp.float32).sum(axis=0)


def contract(left, right):
    return lax.dot_general(
        left, right, (((1,), (1,)), ((), ())), preferred_element_type=jnp.float32
    )


def cleaned(block, live, onehot_full, sums, counts):
    means = sums / jnp.maximum(counts, 1.0)
    spread = lax.dot_general(
        means, onehot_full, (((1,), (1,)), ((), ())), precision=lax.Precision.HIGHEST
    )
    return (live.astype(jnp.float32)[None, :] * (block.astype(jnp.float32) - spread)).astype(
        jnp.bfloat16
    )


def per_device(slopes, valid, sensor_map, reconstructor, fitting):
    width_local = slopes.shape[1]
    start = lax.axis_index("sens") * width_local
    parity = (lax.iota(jnp.int32, width_local) + start) % 2
    group = sensor_map * 2 + parity
    labels = lax.iota(jnp.int32, 2 * SENSORS)
    onehot_full = (group[:, None] == labels[None, :]).astype(jnp.float32)
    onehot_low = onehot_full.astype(jnp.bfloat16)
    live = valid.astype(jnp.bfloat16)
    count_terms = jnp.dot(live[None, :], onehot_low, preferred_element_type=jnp.float32)[0]
    whole = lax.all_gather(slopes, "layer", axis=0, tiled=True)
    masked = whole * live[None, :]
    sums = jnp.dot(masked, onehot_low, preferred_element_type=jnp.float32)
    sums, counts = (
        taken_together(sums.astype(jnp.bfloat16), "sens").astype(jnp.float32),
        taken_together(count_terms.astype(jnp.bfloat16), "sens").astype(jnp.float32),
    )
    clean = cleaned(whole, live, onehot_full, sums, counts)
    partial_points = contract(clean, reconstructor)
    points = summed_on_arrival(partial_points.astype(jnp.bfloat16), "sens", 0).astype(jnp.bfloat16)
    partial_commands = contract(points, lax.all_gather(fitting, "sens", axis=0, tiled=True))
    return summed_on_arrival(partial_commands.astype(jnp.bfloat16), "layer", 0)


def solution(mesh):
    placed = (P("layer", "sens"), P("sens"), P("sens"), P("layer", "sens"), P("sens", "layer"))
    return jax.shard_map(
        per_device,
        mesh=mesh,
        in_specs=placed,
        out_specs=P(("sens", "layer"), None),
        check_vma=False,
    )
```

profile of v0, /device:TPU:0, one launch (start us, length us, event | category | flops | bytes accessed | tf_op | source)
XLA Modules:
  0.0 284.0 jit_solution(14590893099064575598)
XLA Ops:
  6.5 0.0 all-gather.4.cloned.1.call-start
  6.5 0.7 all-gather.4.cloned.1.call-update
  7.3 0.0 all-gather.6.cloned.1.call-start
  7.3 0.7 all-gather.6.cloned.1.call-update
  8.0 0.8 fusion.17
  8.8 0.2 fusion.6
  9.0 10.5 %all_to_all.21 = bf16[8,1,12]{2,1,0:T(2,128)(2,1)S(1)} all-to-all(bf16[8,1,12]{2,1,0:T(2,128)(2,1)S(1)} %broadcast_in_dim.5), channel_id=1, replica_groups=mesh['sens'=8,'layer'=16] {'sens'}, dimensions={0} | all-to-all | bytes 384 | tf_op jit(solution)/shard_map/all_to_all | solution.py:11
  19.5 102.3 %all-gather.4.cloned.1.call-done = bf16[1024,7950]{1,0:T(8,128)(2,1)} async-done(((bf16[64,7950]{1,0:T(8,128)(2,1)}), bf16[1024,7950]{1,0:T(8,128)(2,1)}) %all-gather.4.cloned.1.call-update) | async-done | bytes 16281616 | tf_op jit(solution)/shard_map/all_gather | solution.py:57
  121.9 10.0 %fusion.3 = bf16[1024,12]{0,1:T(8,128)(2,1)S(1)} fusion(bf16[1024,7950]{1,0:T(8,128)(2,1)} %all-gather.4.cloned.1.call-done, bf16[7950]{0:T(1024)(128)(2,1)S(1)} %get-tuple-element.6, s32[7950]{0:T(1024)S(1)} %get-tuple-element.7), kind=kOutput, calls=%fused_computation.8 | convolution fusion | flops 203818496 | bytes 16353876 | tf_op jit(solution)/shard_map/dot_general | solution.py:59
  131.9 0.8 broadcast_in_dim.4
  132.7 4.4 %all-to-all-start = ((bf16[8,1024,12]{1,2,0:T(8,128)(2,1)}), bf16[8,1024,12]{1,2,0:T(8,128)(2,1)S(1)}, u32[]{:S(2)}, u32[]{:S(2)}) async-start(bf16[8,1024,12]{1,2,0:T(8,128)(2,1)} %broadcast_in_dim.4), calls=%async_computation | async-start | bytes 524288 | tf_op jit(solution)/shard_map/all_to_all | solution.py:11
  137.1 22.4 %copy.24 = bf16[1024,7950]{0,1:T(8,128)(2,1)} copy(bf16[1024,7950]{1,0:T(8,128)(2,1)} %all-gather.4.cloned.1.call-done) | data formatting | bytes 32563200 | tf_op jit(solution)/shard_map/all_gather | solution.py:57
  159.5 0.0 all-to-all-done
  159.6 19.0 %multiply_convert_fusion = bf16[1024,7950]{0,1:T(8,128)(2,1)S(1)} fusion(bf16[1024,7950]{0,1:T(8,128)(2,1)} %copy.24, f32[7950]{0:T(1024)S(1)} %get-tuple-element.5, s32[7950]{0:T(1024)S(1)} %get-tuple-element.7, f32[1024,12]{0,1:T(8,128)S(1)} %convert_reduce_fusion.1, f32[12]{0:T(128)S(1)} %broadcast_maximum_fusion), kind=kOutput, calls=%fused_computation | convolution fusion | flops 1204946048 | bytes 32676000 | tf_op jit(solution)/shard_map/dot_general | solution.py:39
  178.5 20.7 %convert_bitcast_fusion = bf16[125,8,8,128]{3,2,1,0:T(8,128)(2,1)S(1)} fusion(bf16[1024,7950]{0,1:T(8,128)(2,1)S(1)} %multiply_convert_fusion, bf16[1000,7950]{1,0:T(8,128)(2,1)} %param.8), kind=kOutput, calls=%fused_computation.7 | convolution fusion | flops 16282624000 | bytes 34229600 | tf_op jit(solution)/shard_map/dot_general | solution.py:32
  199.3 1.6 copy.33
  200.9 4.7 %all-to-all-start.2 = ((bf16[8,128,1000]{1,2,0:T(8,128)(2,1)}), bf16[8,128,1000]{1,2,0:T(8,128)(2,1)S(1)}, u32[]{:S(2)}, u32[]{:S(2)}) async-start(bf16[8,128,1000]{1,2,0:T(8,128)(2,1)} %bitcast.16), calls=%async_computation.2 | async-start | bytes 4096000 | tf_op jit(solution)/shard_map/all_to_all | solution.py:27
  205.7 2.3 all-gather.6.cloned.1.call-done
  208.0 20.5 %reshape.30 = bf16[7800,1000]{1,0:T(8,128)(2,1)} reshape(bf16[8,975,1000]{2,1,0:T(8,128)(2,1)} %all-gather.6.cloned.1.call-done) | data formatting | bytes 31200000
  228.5 3.8 %all-to-all-done.2 = bf16[8,128,1000]{1,2,0:T(8,128)(2,1)S(1)} async-done(((bf16[8,128,1000]{1,2,0:T(8,128)(2,1)}), bf16[8,128,1000]{1,2,0:T(8,128)(2,1)S(1)}, u32[]{:S(2)}, u32[]{:S(2)}) %all-to-all-start.2) | async-done | bytes 2048032 | tf_op jit(solution)/shard_map/all_to_all | solution.py:27
  232.3 0.4 reduce_sum.41
  232.7 9.3 %convolution_convert_fusion = bf16[128,7800]{0,1:T(8,128)(2,1)} fusion(bf16[128,1000]{0,1:T(8,128)(2,1)S(1)} %reduce_sum.41, bf16[7800,1000]{1,0:T(8,128)(2,1)} %reshape.30), kind=kOutput, calls=%fused_computation.3 | convolution fusion | flops 1997798400 | bytes 17852800 | tf_op jit(solution)/shard_map/dot_general | solution.py:32
  242.0 2.9 %copy.28 = bf16[128,7800]{1,0:T(8,128)(2,1)S(1)} copy(bf16[128,7800]{0,1:T(8,128)(2,1)} %convolution_convert_fusion) | data formatting | bytes 3993600 | tf_op jit(solution)/shard_map/convert_element_type | solution.py:68
  244.9 31.2 %all_to_all.22 = bf16[16,8,7800]{2,1,0:T(8,128)(2,1)S(1)} all-to-all(bf16[16,8,7800]{2,1,0:T(8,128)(2,1)S(1)} %bitcast.17), channel_id=1, replica_groups=mesh['sens'=8,'layer'=16] {'layer'}, dimensions={0} | all-to-all | bytes 3993600 | tf_op jit(solution)/shard_map/all_to_all | solution.py:27
  276.2 1.0 convert_reduce_fusion
  (5 shorter events, 0.1 us)
Async XLA Ops:
  6.5 115.3 %all-gather.4.cloned.1.call-start = ((), (), s32[]{:S(2)}) async-start(), calls=%async_computation.4 | async-start | bytes 17547264 | tf_op jit(solution)/shard_map/all_gather | solution.py:57
  7.3 200.7 %all-gather.6.cloned.1.call-start = ((), (), s32[]{:S(2)}) async-start(), calls=%async_computation.5 | async-start | bytes 17989632 | tf_op jit(solution)/shard_map/all_gather | solution.py:67
  132.7 26.8 %all-to-all-start = ((bf16[8,1024,12]{1,2,0:T(8,128)(2,1)}), bf16[8,1024,12]{1,2,0:T(8,128)(2,1)S(1)}, u32[]{:S(2)}, u32[]{:S(2)}) async-start(bf16[8,1024,12]{1,2,0:T(8,128)(2,1)} %broadcast_in_dim.4), calls=%async_computation | async-start | bytes 524288 | tf_op jit(solution)/shard_map/all_to_all | solution.py:11
  200.9 31.4 %all-to-all-start.2 = ((bf16[8,128,1000]{1,2,0:T(8,128)(2,1)}), bf16[8,128,1000]{1,2,0:T(8,128)(2,1)S(1)}, u32[]{:S(2)}, u32[]{:S(2)}) async-start(bf16[8,128,1000]{1,2,0:T(8,128)(2,1)} %bitcast.16), calls=%async_computation.2 | async-start | bytes 4096000 | tf_op jit(solution)/shard_map/all_to_all | solution.py:27
Sparse Core Ops, SparseCore 0:
  9.5 112.3 all-gather.3
  123.5 84.3 all-gather.5
where the time goes:
time: 285 us; the launch traced here: 284 us
  waiting for transfers between devices  110 us (39%)
  matrix products  59.2 us (21%)
  local copies, waits for them, and re-layouts  48.3 us (17%)
  blocking collectives  41.7 us (15%)
  between operations  13.5 us (5%)
  starting transfers between devices  9.2 us (3%)
    all_gather x1, waiting for transfers between devices, per_device(): whole = lax.all_gather(slopes, 'layer', axis=0, tiled=True)  102 us
    all_to_all x1, blocking collectives, summed_on_arrival(): lax.all_to_all(blocks, axis, split_axis=0, concat_axis=0, tiled=True)  31.2 us
    dot_general x2, matrix products, contract(): lax.dot_general(left, right, (((1,), (1,)), ((), ())), preferred_element_...  30 us
    all_gather x1, local copies, waits for them, and re-layouts, per_device(): whole = lax.all_gather(slopes, 'layer', axis=0, tiled=True)  22.4 us
    unnamed x1, local copies, waits for them, and re-layouts  20.5 us
    dot_general x1, matrix products, cleaned(): lax.dot_general(means, onehot_full, (((1,), (1,)), ((), ())), precision=l...  19 us
    all_to_all x1, blocking collectives, copy_for_each(): lax.all_to_all(jnp.broadcast_to(x[None], (length, *x.shape)), axis, 0, 0,...  10.5 us
    dot_general x1, matrix products, per_device(): sums = jnp.dot(masked, onehot_low, preferred_element_type=jnp.float32)  10 us
  transfers between devices with their start and end apart: 4, of which 3 were waited for; matrix products, arithmetic and copies ran while one was open for 34% of the time, Pallas kernels for 0%

commit v1 on v0

--- a/solution.py
+++ b/solution.py
@@ -54,7 +54,22 @@
     onehot_low = onehot_full.astype(jnp.bfloat16)
     live = valid.astype(jnp.bfloat16)
     count_terms = jnp.dot(live[None, :], onehot_low, preferred_element_type=jnp.float32)[0]
-    whole = lax.all_gather(slopes, "layer", axis=0, tiled=True)
+    size, index, span = (lax.axis_size("layer"), lax.axis_index("layer"), slopes.shape[0])
+    ahead = [(i, (i + 1) % size) for i in range(size)]
+    backward = [(i, (i - 1) % size) for i in range(size)]
+    out = jnp.zeros((*slopes.shape[:0], size * span, *slopes.shape[0 + 1 :]), slopes.dtype)
+    out = lax.dynamic_update_slice_in_dim(out, slopes, index * span, axis=0)
+    from_left = from_right = slopes
+    middle = size // 2
+    for step in range(1, middle + 1):
+        from_left = lax.ppermute(from_left, "layer", ahead)
+        out = lax.dynamic_update_slice_in_dim(out, from_left, (index - step) % size * span, axis=0)
+        if step < size - middle:
+            from_right = lax.ppermute(from_right, "layer", backward)
+            out = lax.dynamic_update_slice_in_dim(
+                out, from_right, (index + step) % size * span, axis=0
+            )
+    whole = out
     masked = whole * live[None, :]
     sums = jnp.dot(masked, onehot_low, preferred_element_type=jnp.float32)
     sums, counts = (

time: 285 us -> 751 us (2.64); the launches traced: 284 us -> 736 us
  local copies, waits for them, and re-layouts: 48.3 us -> 399 us
  waiting for transfers between devices: 110 us -> 149 us
  starting transfers between devices: 9.2 us -> 47.6 us
  blocking collectives: 41.7 us -> 63.2 us
    dynamic_update_slice x0 -> x16, local copies, waits for them, and re-layouts: none -> 331 us  [the longest x8 165 us: per_device(): lax.dynamic_update_slice_in_dim(out, from_left, (index - step) % size * s...]
    ppermute x0 -> x15, waiting for transfers between devices: none -> 141 us  [the longest x8 141 us: per_device(): from_left = lax.ppermute(from_left, 'layer', ahead)]
    all_gather x1 -> x0, waiting for transfers between devices: 102 us -> none  [per_device(): whole = lax.all_gather(slopes, 'layer', axis=0, tiled=True)]
    ppermute x0 -> x15, starting transfers between devices: none -> 37.5 us  [the longest x7 35.8 us: per_device(): from_right = lax.ppermute(from_right, 'layer', backward)]
    ppermute x0 -> x15, local copies, waits for them, and re-layouts: none -> 34.4 us  [the longest x8 17.9 us: per_device(): from_left = lax.ppermute(from_left, 'layer', ahead)]
    all_to_all x1 -> x2, blocking collectives: 31.2 us -> 63.2 us  [summed_on_arrival(): lax.all_to_all(blocks, axis, split_axis=0, concat_axis=0, tiled=True)]
    all_gather x1 -> x0, local copies, waits for them, and re-layouts: 22.4 us -> none  [per_device(): whole = lax.all_gather(slopes, 'layer', axis=0, tiled=True)]
    all_to_all x1 -> x0, blocking collectives: 10.5 us -> none  [copy_for_each(): lax.all_to_all(jnp.broadcast_to(x[None], (length, *x.shape)), axis, 0, 0,...]
  transfers between devices with their start and end apart: 4 -> 18, of which waited for: 3 -> 8; matrix products, arithmetic and copies ran while one was open for 34% -> 58% of each run, Pallas kernels for 0% -> 0%
where the time goes in v1:
time: 751 us; the launch traced here: 736 us
  local copies, waits for them, and re-layouts  399 us (53%)
  waiting for transfers between devices  149 us (20%)
  blocking collectives  63.2 us (8%)
  matrix products  60.3 us (8%)
  starting transfers between devices  47.6 us (6%)
  between operations  14.3 us (2%)
    dynamic_update_slice x8, local copies, waits for them, and re-layouts, per_device(): lax.dynamic_update_slice_in_dim(out, from_left, (index - step) % size * s...  165 us
    dynamic_update_slice x7, local copies, waits for them, and re-layouts, per_device(): lax.dynamic_update_slice_in_dim(out, from_right, (index + step) % size *...  147 us
    ppermute x8, waiting for transfers between devices, per_device(): from_left = lax.ppermute(from_left, 'layer', ahead)  141 us
    all_to_all x2, blocking collectives, summed_on_arrival(): lax.all_to_all(blocks, axis, split_axis=0, concat_axis=0, tiled=True)  63.2 us
    ppermute x7, starting transfers between devices, per_device(): from_right = lax.ppermute(from_right, 'layer', backward)  35.8 us
    dot_general x2, matrix products, contract(): lax.dot_general(left, right, (((1,), (1,)), ((), ())), preferred_element_...  35.2 us
    unnamed x24, local copies, waits for them, and re-layouts  22.9 us
    dynamic_update_slice x1, local copies, waits for them, and re-layouts, per_device(): out = lax.dynamic_update_slice_in_dim(out, slopes, index * span, axis=0)  19.4 us
  transfers between devices with their start and end apart: 18, of which 8 were waited for; matrix products, arithmetic and copies ran while one was open for 58% of the time, Pallas kernels for 0%

profile of v1, /device:TPU:0, one launch (start us, length us, event | category | flops | bytes accessed | tf_op | source)
XLA Modules:
  0.0 736.4 jit_solution(10150333326073654602)
XLA Ops:
  6.5 0.7 all-gather.3.cloned.1.call-update
  7.3 1.6 collective-permute-start
  8.9 3.8 collective-permute-start.1
  12.7 22.9 %collective-permute-done = bf16[64,7950]{1,0:T(8,128)(2,1)S(1)} collective-permute-done((bf16[64,7950]{1,0:T(8,128)(2,1)}, bf16[64,7950]{1,0:T(8,128)(2,1)S(1)}, u32[]{:S(2)}, u32[]{:S(2)}) %collective-permute-start) | collective-permute-done | bytes 1017632 | tf_op jit(solution)/shard_map/ppermute | solution.py:65
  35.7 5.3 collective-permute-start.3
  41.0 21.9 %collective-permute-done.2 = bf16[64,7950]{1,0:T(8,128)(2,1)S(1)} collective-permute-done((bf16[64,7950]{1,0:T(8,128)(2,1)S(1)}, bf16[64,7950]{1,0:T(8,128)(2,1)S(1)}, u32[]{:S(2)}, u32[]{:S(2)}) %collective-permute-start.2) | collective-permute-done | bytes 1017632 | tf_op jit(solution)/shard_map/ppermute | solution.py:65
  62.9 5.3 collective-permute-start.5
  68.3 21.0 %collective-permute-done.4 = bf16[64,7950]{1,0:T(8,128)(2,1)S(1)} collective-permute-done((bf16[64,7950]{1,0:T(8,128)(2,1)S(1)}, bf16[64,7950]{1,0:T(8,128)(2,1)S(1)}, u32[]{:S(2)}, u32[]{:S(2)}) %collective-permute-start.4) | collective-permute-done | bytes 1017632 | tf_op jit(solution)/shard_map/ppermute | solution.py:65
  89.3 5.3 collective-permute-start.7
  94.6 20.1 %collective-permute-done.6 = bf16[64,7950]{1,0:T(8,128)(2,1)S(1)} collective-permute-done((bf16[64,7950]{1,0:T(8,128)(2,1)S(1)}, bf16[64,7950]{1,0:T(8,128)(2,1)S(1)}, u32[]{:S(2)}, u32[]{:S(2)}) %collective-permute-start.6) | collective-permute-done | bytes 1017632 | tf_op jit(solution)/shard_map/ppermute | solution.py:65
  114.7 5.3 collective-permute-start.9
  120.0 19.1 %collective-permute-done.8 = bf16[64,7950]{1,0:T(8,128)(2,1)S(1)} collective-permute-done((bf16[64,7950]{1,0:T(8,128)(2,1)S(1)}, bf16[64,7950]{1,0:T(8,128)(2,1)S(1)}, u32[]{:S(2)}, u32[]{:S(2)}) %collective-permute-start.8) | collective-permute-done | bytes 1017632 | tf_op jit(solution)/shard_map/ppermute | solution.py:65
  139.2 5.3 collective-permute-start.11
  144.5 18.2 %collective-permute-done.10 = bf16[64,7950]{1,0:T(8,128)(2,1)S(1)} collective-permute-done((bf16[64,7950]{1,0:T(8,128)(2,1)S(1)}, bf16[64,7950]{1,0:T(8,128)(2,1)S(1)}, u32[]{:S(2)}, u32[]{:S(2)}) %collective-permute-start.10) | collective-permute-done | bytes 1017632 | tf_op jit(solution)/shard_map/ppermute | solution.py:65
  162.7 5.3 collective-permute-start.13
  168.1 17.6 %collective-permute-done.12 = bf16[64,7950]{1,0:T(8,128)(2,1)S(1)} collective-permute-done((bf16[64,7950]{1,0:T(8,128)(2,1)S(1)}, bf16[64,7950]{1,0:T(8,128)(2,1)S(1)}, u32[]{:S(2)}, u32[]{:S(2)}) %collective-permute-start.12) | collective-permute-done | bytes 1017632 | tf_op jit(solution)/shard_map/ppermute | solution.py:65
  185.8 0.8 fusion.20
  186.6 0.8 fusion.15
  188.2 5.3 all-to-all-start.1
  193.6 2.4 copy.71
  196.2 5.8 broadcast_in_dim.6
  202.0 19.4 %dynamic_update_slice.48 = bf16[1024,7950]{0,1:T(8,128)(2,1)} dynamic-update-slice(bf16[1024,7950]{0,1:T(8,128)(2,1)} %broadcast_in_dim.6, bf16[64,7950]{0,1:T(8,128)(2,1)S(1)} %copy.71, s32[]{:T(128)S(6)} %select_n.117, s32[]{:T(128)} %constant.111.clone.1) | dynamic-update-slice | bytes 2035204 | tf_op jit(solution)/shard_map/dynamic_update_slice | solution.py:61
  221.4 2.4 copy.72
  223.8 21.4 %dynamic_update_slice.49 = bf16[1024,7950]{0,1:T(8,128)(2,1)} dynamic-update-slice(bf16[1024,7950]{0,1:T(8,128)(2,1)} %dynamic_update_slice.48, bf16[64,7950]{0,1:T(8,128)(2,1)S(1)} %copy.72, s32[]{:T(128)S(6)} %select_n.119, s32[]{:T(128)} %constant.111.clone.1) | dynamic-update-slice | bytes 2035204 | tf_op jit(solution)/shard_map/dynamic_update_slice | solution.py:66
  245.2 2.4 copy.73
  247.6 22.3 %dynamic_update_slice.50 = bf16[1024,7950]{0,1:T(8,128)(2,1)} dynamic-update-slice(bf16[1024,7950]{0,1:T(8,128)(2,1)} %dynamic_update_slice.49, bf16[64,7950]{0,1:T(8,128)(2,1)S(1)} %copy.73, s32[]{:T(128)S(6)} %select_n.121, s32[]{:T(128)} %constant.111.clone.1) | dynamic-update-slice | bytes 2035204 | tf_op jit(solution)/shard_map/dynamic_update_slice | solution.py:69
  269.8 2.4 copy.74
  272.2 18.0 %dynamic_update_slice.51 = bf16[1024,7950]{0,1:T(8,128)(2,1)} dynamic-update-slice(bf16[1024,7950]{0,1:T(8,128)(2,1)} %dynamic_update_slice.50, bf16[64,7950]{0,1:T(8,128)(2,1)S(1)} %copy.74, s32[]{:T(128)S(6)} %select_n.123, s32[]{:T(128)} %constant.111.clone.1) | dynamic-update-slice | bytes 2035204 | tf_op jit(solution)/shard_map/dynamic_update_slice | solution.py:66
  290.2 2.4 copy.75
  292.6 19.3 %dynamic_update_slice.52 = bf16[1024,7950]{0,1:T(8,128)(2,1)} dynamic-update-slice(bf16[1024,7950]{0,1:T(8,128)(2,1)} %dynamic_update_slice.51, bf16[64,7950]{0,1:T(8,128)(2,1)S(1)} %copy.75, s32[]{:T(128)S(6)} %select_n.125, s32[]{:T(128)} %constant.111.clone.1) | dynamic-update-slice | bytes 2035204 | tf_op jit(solution)/shard_map/dynamic_update_slice | solution.py:69
  312.0 2.4 copy.76
  314.3 22.2 %dynamic_update_slice.53 = bf16[1024,7950]{0,1:T(8,128)(2,1)} dynamic-update-slice(bf16[1024,7950]{0,1:T(8,128)(2,1)} %dynamic_update_slice.52, bf16[64,7950]{0,1:T(8,128)(2,1)S(1)} %copy.76, s32[]{:T(128)S(6)} %select_n.127, s32[]{:T(128)} %constant.111.clone.1) | dynamic-update-slice | bytes 2035204 | tf_op jit(solution)/shard_map/dynamic_update_slice | solution.py:66
  336.6 2.4 copy.77
  338.9 22.3 %dynamic_update_slice.54 = bf16[1024,7950]{0,1:T(8,128)(2,1)} dynamic-update-slice(bf16[1024,7950]{0,1:T(8,128)(2,1)} %dynamic_update_slice.53, bf16[64,7950]{0,1:T(8,128)(2,1)S(1)} %copy.77, s32[]{:T(128)S(6)} %select_n.129, s32[]{:T(128)} %constant.111.clone.1) | dynamic-update-slice | bytes 2035204 | tf_op jit(solution)/shard_map/dynamic_update_slice | solution.py:69
  361.2 2.4 copy.78
  363.5 19.4 %dynamic_update_slice.55 = bf16[1024,7950]{0,1:T(8,128)(2,1)} dynamic-update-slice(bf16[1024,7950]{0,1:T(8,128)(2,1)} %dynamic_update_slice.54, bf16[64,7950]{0,1:T(8,128)(2,1)S(1)} %copy.78, s32[]{:T(128)S(6)} %select_n.131, s32[]{:T(128)} %constant.111.clone.1) | dynamic-update-slice | bytes 2035204 | tf_op jit(solution)/shard_map/dynamic_update_slice | solution.py:66
  382.9 2.4 copy.79
  385.3 19.4 %dynamic_update_slice.56 = bf16[1024,7950]{0,1:T(8,128)(2,1)} dynamic-update-slice(bf16[1024,7950]{0,1:T(8,128)(2,1)} %dynamic_update_slice.55, bf16[64,7950]{0,1:T(8,128)(2,1)S(1)} %copy.79, s32[]{:T(128)S(6)} %select_n.133, s32[]{:T(128)} %constant.111.clone.1) | dynamic-update-slice | bytes 2035204 | tf_op jit(solution)/shard_map/dynamic_update_slice | solution.py:69
  404.6 2.4 copy.80
  407.0 22.3 %dynamic_update_slice.57 = bf16[1024,7950]{0,1:T(8,128)(2,1)} dynamic-update-slice(bf16[1024,7950]{0,1:T(8,128)(2,1)} %dynamic_update_slice.56, bf16[64,7950]{0,1:T(8,128)(2,1)S(1)} %copy.80, s32[]{:T(128)S(6)} %select_n.135, s32[]{:T(128)} %constant.111.clone.1) | dynamic-update-slice | bytes 2035204 | tf_op jit(solution)/shard_map/dynamic_update_slice | solution.py:66
  429.3 2.4 copy.81
  431.6 22.3 %dynamic_update_slice.58 = bf16[1024,7950]{0,1:T(8,128)(2,1)} dynamic-update-slice(bf16[1024,7950]{0,1:T(8,128)(2,1)} %dynamic_update_slice.57, bf16[64,7950]{0,1:T(8,128)(2,1)S(1)} %copy.81, s32[]{:T(128)S(6)} %select_n.137, s32[]{:T(128)} %constant.111.clone.1) | dynamic-update-slice | bytes 2035204 | tf_op jit(solution)/shard_map/dynamic_update_slice | solution.py:69
  453.9 2.4 copy.82
  456.2 19.4 %dynamic_update_slice.59 = bf16[1024,7950]{0,1:T(8,128)(2,1)} dynamic-update-slice(bf16[1024,7950]{0,1:T(8,128)(2,1)} %dynamic_update_slice.58, bf16[64,7950]{0,1:T(8,128)(2,1)S(1)} %copy.82, s32[]{:T(128)S(6)} %select_n.139, s32[]{:T(128)} %constant.111.clone.1) | dynamic-update-slice | bytes 2035204 | tf_op jit(solution)/shard_map/dynamic_update_slice | solution.py:66
  475.6 2.4 copy.83
  478.0 19.3 %dynamic_update_slice.60 = bf16[1024,7950]{0,1:T(8,128)(2,1)} dynamic-update-slice(bf16[1024,7950]{0,1:T(8,128)(2,1)} %dynamic_update_slice.59, bf16[64,7950]{0,1:T(8,128)(2,1)S(1)} %copy.83, s32[]{:T(128)S(6)} %select_n.141, s32[]{:T(128)} %constant.111.clone.1) | dynamic-update-slice | bytes 2035204 | tf_op jit(solution)/shard_map/dynamic_update_slice | solution.py:69
  497.3 1.5 copy.84
  498.8 22.4 %dynamic_update_slice.61 = bf16[1024,7950]{0,1:T(8,128)(2,1)} dynamic-update-slice(bf16[1024,7950]{0,1:T(8,128)(2,1)} %dynamic_update_slice.60, bf16[64,7950]{0,1:T(8,128)(2,1)S(1)} %copy.84, s32[]{:T(128)S(6)} %select_n.143, s32[]{:T(128)} %constant.111.clone.1) | dynamic-update-slice | bytes 2035204 | tf_op jit(solution)/shard_map/dynamic_update_slice | solution.py:66
  521.2 2.4 copy.85
  523.6 22.3 %dynamic_update_slice.62 = bf16[1024,7950]{0,1:T(8,128)(2,1)} dynamic-update-slice(bf16[1024,7950]{0,1:T(8,128)(2,1)} %dynamic_update_slice.61, bf16[64,7950]{0,1:T(8,128)(2,1)S(1)} %copy.85, s32[]{:T(128)S(6)} %select_n.145, s32[]{:T(128)} %constant.111.clone.1) | dynamic-update-slice | bytes 2035204 | tf_op jit(solution)/shard_map/dynamic_update_slice | solution.py:69
  545.9 2.4 copy.86
  548.3 19.4 %dynamic_update_slice.63 = bf16[1024,7950]{0,1:T(8,128)(2,1)} dynamic-update-slice(bf16[1024,7950]{0,1:T(8,128)(2,1)} %dynamic_update_slice.62, bf16[64,7950]{0,1:T(8,128)(2,1)S(1)} %copy.86, s32[]{:T(128)S(6)} %select_n.147, s32[]{:T(128)} %constant.111.clone.1) | dynamic-update-slice | bytes 2035204 | tf_op jit(solution)/shard_map/dynamic_update_slice | solution.py:66
  567.7 8.0 %fusion.5 = bf16[1024,12]{0,1:T(8,128)(2,1)S(1)} fusion(bf16[1024,7950]{0,1:T(8,128)(2,1)} %dynamic_update_slice.63, bf16[7950]{0:T(1024)(128)(2,1)S(1)} %get-tuple-element.6, s32[7950]{0:T(1024)S(1)} %fusion.15), kind=kOutput, calls=%fused_computation.10 | convolution fusion | flops 203818496 | bytes 16353876 | tf_op jit(solution)/shard_map/dot_general | solution.py:74
  575.7 0.7 broadcast_in_dim.7
  576.5 4.8 all-to-all-start
  581.3 7.5 %all-to-all-done = bf16[8,1024,12]{1,2,0:T(8,128)(2,1)S(1)} async-done(((bf16[8,1024,12]{1,2,0:T(8,128)(2,1)}), bf16[8,1024,12]{1,2,0:T(8,128)(2,1)S(1)}, u32[]{:S(2)}, u32[]{:S(2)}) %all-to-all-start) | async-done | bytes 196640 | tf_op jit(solution)/shard_map/all_to_all | solution.py:11
  588.9 16.9 %fusion.9 = f32[1024,7950]{0,1:T(8,128)} fusion(s32[7950]{0:T(1024)S(1)} %fusion.15, f32[1024,12]{0,1:T(8,128)S(1)} %convert_reduce_fusion.1, f32[12]{0:T(128)S(1)} %broadcast_maximum_fusion), kind=kOutput, calls=%fused_computation.16 | convolution fusion | flops 1172382848 | bytes 32644200 | tf_op jit(solution)/shard_map/dot_general | solution.py:39
  605.8 26.0 %convert_bitcast_fusion = bf16[125,8,8,128]{3,2,1,0:T(8,128)(2,1)S(1)} fusion(bf16[1000,7950]{1,0:T(8,128)(2,1)} %param.8, f32[1024,7950]{0,1:T(8,128)} %fusion.9, bf16[1024,7950]{0,1:T(8,128)(2,1)} %dynamic_update_slice.63, f32[7950]{0:T(1024)S(1)} %get-tuple-element.5), kind=kOutput, calls=%fused_computation.9 | convolution fusion | flops 16315187200 | bytes 66824600 | tf_op jit(solution)/shard_map/dot_general | solution.py:32
  632.1 29.6 %all_to_all.21 = bf16[8,128,1000]{1,2,0:T(8,128)(2,1)S(1)} all-to-all(bf16[8,128,1000]{1,2,0:T(8,128)(2,1)S(1)} %bitcast.15), channel_id=1, replica_groups=mesh['sens'=8,'layer'=16] {'sens'}, dimensions={0} | all-to-all | bytes 4096000 | tf_op jit(solution)/shard_map/all_to_all | solution.py:27
  662.1 20.5 %reshape.30 = bf16[7800,1000]{1,0:T(8,128)(2,1)} reshape(bf16[8,975,1000]{2,1,0:T(8,128)(2,1)} %all-gather.3.cloned.1.call-done) | data formatting | bytes 31200000
  682.6 9.2 %convolution_convert_fusion = bf16[128,7800]{0,1:T(8,128)(2,1)} fusion(bf16[128,1000]{0,1:T(8,128)(2,1)S(1)} %reduce_sum.41, bf16[7800,1000]{1,0:T(8,128)(2,1)} %reshape.30), kind=kOutput, calls=%fused_computation.5 | convolution fusion | flops 1997798400 | bytes 17852800 | tf_op jit(solution)/shard_map/dot_general | solution.py:32
  691.9 2.9 copy.90
  694.8 33.5 %all_to_all.22 = bf16[16,8,7800]{2,1,0:T(8,128)(2,1)S(1)} all-to-all(bf16[16,8,7800]{2,1,0:T(8,128)(2,1)S(1)} %bitcast.16), channel_id=1, replica_groups=mesh['sens'=8,'layer'=16] {'layer'}, dimensions={0} | all-to-all | bytes 3993600 | tf_op jit(solution)/shard_map/all_to_all | solution.py:27
  728.3 1.0 convert_reduce_fusion
  (48 shorter events, 1.8 us)
Async XLA Ops:
  6.5 655.6 %all-gather.3.cloned.1.call-start = ((), (), s32[]{:S(2)}) async-start(), calls=%async_computation.4 | async-start | bytes 17989632 | tf_op jit(solution)/shard_map/all_gather | solution.py:82
  7.3 28.4 %collective-permute-start = (bf16[64,7950]{1,0:T(8,128)(2,1)}, bf16[64,7950]{1,0:T(8,128)(2,1)S(1)}, u32[]{:S(2)}, u32[]{:S(2)}) collective-permute-start(bf16[64,7950]{1,0:T(8,128)(2,1)} %param.5), channel_id=1, source_target_pairs={{0,1},{1,2},{2,3},{3,4},{4,5},{5,6},{6,7},{7,8},{8,9},{9,10},{10,1... | collective-permute-start | bytes 3052808 | tf_op jit(solution)/shard_map/ppermute | solution.py:65
  8.9 26.7 %collective-permute-start.1 = (bf16[64,7950]{1,0:T(8,128)(2,1)}, bf16[64,7950]{1,0:T(8,128)(2,1)S(1)}, u32[]{:S(2)}, u32[]{:S(2)}) collective-permute-start(bf16[64,7950]{1,0:T(8,128)(2,1)} %param.5), channel_id=1, source_target_pairs={{0,15},{1,0},{2,1},{3,2},{4,3},{5,4},{6,5},{7,6},{8,7},{9,8},{10,9... | collective-permute-start | bytes 3052808 | tf_op jit(solution)/shard_map/ppermute | solution.py:68
  35.6 150.1 %copy-start.2 = (bf16[64,7950]{1,0:T(8,128)(2,1)}, bf16[64,7950]{1,0:T(8,128)(2,1)S(1)}, u32[]{:S(2)}) copy-start(bf16[64,7950]{1,0:T(8,128)(2,1)S(1)} %collective-permute-done) | copy-start | bytes 3052804
  35.6 27.3 %collective-permute-start.2 = (bf16[64,7950]{1,0:T(8,128)(2,1)S(1)}, bf16[64,7950]{1,0:T(8,128)(2,1)S(1)}, u32[]{:S(2)}, u32[]{:S(2)}) collective-permute-start(bf16[64,7950]{1,0:T(8,128)(2,1)S(1)} %collective-permute-done), channel_id=1, source_target_pairs={{0,1},{1,2},{2,3},{3,4},{4,5},{5,6},{6,7},{7,8},{8,9},{9,10},{10,1... | collective-permute-start | bytes 3052808 | tf_op jit(solution)/shard_map/ppermute | solution.py:65
  35.6 150.1 %copy-start = (bf16[64,7950]{1,0:T(8,128)(2,1)}, bf16[64,7950]{1,0:T(8,128)(2,1)S(1)}, u32[]{:S(2)}) copy-start(bf16[64,7950]{1,0:T(8,128)(2,1)S(1)} %collective-permute-done.1) | copy-start | bytes 3052804
  35.7 27.2 %collective-permute-start.3 = (bf16[64,7950]{1,0:T(8,128)(2,1)S(1)}, bf16[64,7950]{1,0:T(8,128)(2,1)S(1)}, u32[]{:S(2)}, u32[]{:S(2)}) collective-permute-start(bf16[64,7950]{1,0:T(8,128)(2,1)S(1)} %collective-permute-done.1), channel_id=1, source_target_pairs={{0,15},{1,0},{2,1},{3,2},{4,3},{5,4},{6,5},{7,6},{8,7},{9,8},{10,9... | collective-permute-start | bytes 3052808 | tf_op jit(solution)/shard_map/ppermute | solution.py:68
  62.9 122.8 %copy-start.1 = (bf16[64,7950]{1,0:T(8,128)(2,1)}, bf16[64,7950]{1,0:T(8,128)(2,1)S(1)}, u32[]{:S(2)}) copy-start(bf16[64,7950]{1,0:T(8,128)(2,1)S(1)} %collective-permute-done.2) | copy-start | bytes 3052804
  62.9 26.3 %collective-permute-start.4 = (bf16[64,7950]{1,0:T(8,128)(2,1)S(1)}, bf16[64,7950]{1,0:T(8,128)(2,1)S(1)}, u32[]{:S(2)}, u32[]{:S(2)}) collective-permute-start(bf16[64,7950]{1,0:T(8,128)(2,1)S(1)} %collective-permute-done.2), channel_id=1, source_target_pairs={{0,1},{1,2},{2,3},{3,4},{4,5},{5,6},{6,7},{7,8},{8,9},{9,10},{10,1... | collective-permute-start | bytes 3052808 | tf_op jit(solution)/shard_map/ppermute | solution.py:65
  62.9 122.8 %copy-start.3 = (bf16[64,7950]{1,0:T(8,128)(2,1)}, bf16[64,7950]{1,0:T(8,128)(2,1)S(1)}, u32[]{:S(2)}) copy-start(bf16[64,7950]{1,0:T(8,128)(2,1)S(1)} %collective-permute-done.3) | copy-start | bytes 3052804
  62.9 26.3 %collective-permute-start.5 = (bf16[64,7950]{1,0:T(8,128)(2,1)S(1)}, bf16[64,7950]{1,0:T(8,128)(2,1)S(1)}, u32[]{:S(2)}, u32[]{:S(2)}) collective-permute-start(bf16[64,7950]{1,0:T(8,128)(2,1)S(1)} %collective-permute-done.3), channel_id=1, source_target_pairs={{0,15},{1,0},{2,1},{3,2},{4,3},{5,4},{6,5},{7,6},{8,7},{9,8},{10,9... | collective-permute-start | bytes 3052808 | tf_op jit(solution)/shard_map/ppermute | solution.py:68
  89.2 96.5 %copy-start.4 = (bf16[64,7950]{1,0:T(8,128)(2,1)}, bf16[64,7950]{1,0:T(8,128)(2,1)S(1)}, u32[]{:S(2)}) copy-start(bf16[64,7950]{1,0:T(8,128)(2,1)S(1)} %collective-permute-done.4) | copy-start | bytes 3052804
  89.2 25.4 %collective-permute-start.6 = (bf16[64,7950]{1,0:T(8,128)(2,1)S(1)}, bf16[64,7950]{1,0:T(8,128)(2,1)S(1)}, u32[]{:S(2)}, u32[]{:S(2)}) collective-permute-start(bf16[64,7950]{1,0:T(8,128)(2,1)S(1)} %collective-permute-done.4), channel_id=1, source_target_pairs={{0,1},{1,2},{2,3},{3,4},{4,5},{5,6},{6,7},{7,8},{8,9},{9,10},{10,1... | collective-permute-start | bytes 3052808 | tf_op jit(solution)/shard_map/ppermute | solution.py:65
  89.3 96.5 %copy-start.5 = (bf16[64,7950]{1,0:T(8,128)(2,1)}, bf16[64,7950]{1,0:T(8,128)(2,1)S(1)}, u32[]{:S(2)}) copy-start(bf16[64,7950]{1,0:T(8,128)(2,1)S(1)} %collective-permute-done.5) | copy-start | bytes 3052804
  89.3 25.4 %collective-permute-start.7 = (bf16[64,7950]{1,0:T(8,128)(2,1)S(1)}, bf16[64,7950]{1,0:T(8,128)(2,1)S(1)}, u32[]{:S(2)}, u32[]{:S(2)}) collective-permute-start(bf16[64,7950]{1,0:T(8,128)(2,1)S(1)} %collective-permute-done.5), channel_id=1, source_target_pairs={{0,15},{1,0},{2,1},{3,2},{4,3},{5,4},{6,5},{7,6},{8,7},{9,8},{10,9... | collective-permute-start | bytes 3052808 | tf_op jit(solution)/shard_map/ppermute | solution.py:68
  114.7 71.1 %copy-start.6 = (bf16[64,7950]{1,0:T(8,128)(2,1)}, bf16[64,7950]{1,0:T(8,128)(2,1)S(1)}, u32[]{:S(2)}) copy-start(bf16[64,7950]{1,0:T(8,128)(2,1)S(1)} %collective-permute-done.6) | copy-start | bytes 3052804
  114.7 24.5 %collective-permute-start.8 = (bf16[64,7950]{1,0:T(8,128)(2,1)S(1)}, bf16[64,7950]{1,0:T(8,128)(2,1)S(1)}, u32[]{:S(2)}, u32[]{:S(2)}) collective-permute-start(bf16[64,7950]{1,0:T(8,128)(2,1)S(1)} %collective-permute-done.6), channel_id=1, source_target_pairs={{0,1},{1,2},{2,3},{3,4},{4,5},{5,6},{6,7},{7,8},{8,9},{9,10},{10,1... | collective-permute-start | bytes 3052808 | tf_op jit(solution)/shard_map/ppermute | solution.py:65
  114.7 71.1 %copy-start.7 = (bf16[64,7950]{1,0:T(8,128)(2,1)}, bf16[64,7950]{1,0:T(8,128)(2,1)S(1)}, u32[]{:S(2)}) copy-start(bf16[64,7950]{1,0:T(8,128)(2,1)S(1)} %collective-permute-done.7) | copy-start | bytes 3052804
  114.7 24.5 %collective-permute-start.9 = (bf16[64,7950]{1,0:T(8,128)(2,1)S(1)}, bf16[64,7950]{1,0:T(8,128)(2,1)S(1)}, u32[]{:S(2)}, u32[]{:S(2)}) collective-permute-start(bf16[64,7950]{1,0:T(8,128)(2,1)S(1)} %collective-permute-done.7), channel_id=1, source_target_pairs={{0,15},{1,0},{2,1},{3,2},{4,3},{5,4},{6,5},{7,6},{8,7},{9,8},{10,9... | collective-permute-start | bytes 3052808 | tf_op jit(solution)/shard_map/ppermute | solution.py:68
  139.2 46.6 %copy-start.8 = (bf16[64,7950]{1,0:T(8,128)(2,1)}, bf16[64,7950]{1,0:T(8,128)(2,1)S(1)}, u32[]{:S(2)}) copy-start(bf16[64,7950]{1,0:T(8,128)(2,1)S(1)} %collective-permute-done.8) | copy-start | bytes 3052804
  139.2 23.6 %collective-permute-start.10 = (bf16[64,7950]{1,0:T(8,128)(2,1)S(1)}, bf16[64,7950]{1,0:T(8,128)(2,1)S(1)}, u32[]{:S(2)}, u32[]{:S(2)}) collective-permute-start(bf16[64,7950]{1,0:T(8,128)(2,1)S(1)} %collective-permute-done.8), channel_id=1, source_target_pairs={{0,1},{1,2},{2,3},{3,4},{4,5},{5,6},{6,7},{7,8},{8,9},{9,10},{10,1... | collective-permute-start | bytes 3052808 | tf_op jit(solution)/shard_map/ppermute | solution.py:65
  139.2 46.6 %copy-start.9 = (bf16[64,7950]{1,0:T(8,128)(2,1)}, bf16[64,7950]{1,0:T(8,128)(2,1)S(1)}, u32[]{:S(2)}) copy-start(bf16[64,7950]{1,0:T(8,128)(2,1)S(1)} %collective-permute-done.9) | copy-start | bytes 3052804
  139.2 23.6 %collective-permute-start.11 = (bf16[64,7950]{1,0:T(8,128)(2,1)S(1)}, bf16[64,7950]{1,0:T(8,128)(2,1)}, u32[]{:S(2)}, u32[]{:S(2)}) collective-permute-start(bf16[64,7950]{1,0:T(8,128)(2,1)S(1)} %collective-permute-done.9), channel_id=1, source_target_pairs={{0,15},{1,0},{2,1},{3,2},{4,3},{5,4},{6,5},{7,6},{8,7},{9,8},{10,9... | collective-permute-start | bytes 3052808 | tf_op jit(solution)/shard_map/ppermute | solution.py:68
  162.7 23.1 %copy-start.10 = (bf16[64,7950]{1,0:T(8,128)(2,1)}, bf16[64,7950]{1,0:T(8,128)(2,1)S(1)}, u32[]{:S(2)}) copy-start(bf16[64,7950]{1,0:T(8,128)(2,1)S(1)} %collective-permute-done.10) | copy-start | bytes 3052804
  162.7 23.0 %collective-permute-start.12 = (bf16[64,7950]{1,0:T(8,128)(2,1)S(1)}, bf16[64,7950]{1,0:T(8,128)(2,1)S(1)}, u32[]{:S(2)}, u32[]{:S(2)}) collective-permute-start(bf16[64,7950]{1,0:T(8,128)(2,1)S(1)} %collective-permute-done.10), channel_id=1, source_target_pairs={{0,1},{1,2},{2,3},{3,4},{4,5},{5,6},{6,7},{7,8},{8,9},{9,10},{10,1... | collective-permute-start | bytes 3052808 | tf_op jit(solution)/shard_map/ppermute | solution.py:65
  162.7 358.5 %collective-permute-start.13 = (bf16[64,7950]{1,0:T(8,128)(2,1)}, bf16[64,7950]{1,0:T(8,128)(2,1)}, u32[]{:S(2)}, u32[]{:S(2)}) collective-permute-start(bf16[64,7950]{1,0:T(8,128)(2,1)} %collective-permute-done.11), channel_id=1, source_target_pairs={{0,15},{1,0},{2,1},{3,2},{4,3},{5,4},{6,5},{7,6},{8,7},{9,8},{10,9... | collective-permute-start | bytes 3052808 | tf_op jit(solution)/shard_map/ppermute | solution.py:68
  185.7 360.2 %collective-permute-start.14 = (bf16[64,7950]{1,0:T(8,128)(2,1)S(1)}, bf16[64,7950]{1,0:T(8,128)(2,1)}, u32[]{:S(2)}, u32[]{:S(2)}) collective-permute-start(bf16[64,7950]{1,0:T(8,128)(2,1)S(1)} %collective-permute-done.12), channel_id=1, source_target_pairs={{0,1},{1,2},{2,3},{3,4},{4,5},{5,6},{6,7},{7,8},{8,9},{9,10},{10,1... | collective-permute-start | bytes 3052808 | tf_op jit(solution)/shard_map/ppermute | solution.py:65
  188.2 33.2 %all-to-all-start.1 = ((bf16[8,1,12]{2,1,0:T(2,128)(2,1)}), bf16[8,1,12]{2,1,0:T(2,128)(2,1)S(1)}, u32[]{:S(2)}, u32[]{:S(2)}) async-start(bf16[8,1,12]{2,1,0:T(2,128)(2,1)} %broadcast_in_dim.8), calls=%async_computation.1 | async-start | bytes 8192 | tf_op jit(solution)/shard_map/all_to_all | solution.py:11
  576.5 12.3 %all-to-all-start = ((bf16[8,1024,12]{1,2,0:T(8,128)(2,1)}), bf16[8,1024,12]{1,2,0:T(8,128)(2,1)S(1)}, u32[]{:S(2)}, u32[]{:S(2)}) async-start(bf16[8,1024,12]{1,2,0:T(8,128)(2,1)} %broadcast_in_dim.7), calls=%async_computation | async-start | bytes 524288 | tf_op jit(solution)/shard_map/all_to_all | solution.py:11
Sparse Core Ops, SparseCore 0:
  9.0 84.3 all-gather.2
